TPU v7x, 32 devices: a whole 2x2x4 slice. The times are simulated.
32 devices in a mesh: ctx: 8 (over y, x, core), wshard: 4 (over z).
Axes of the slice: x: 2, y: 2, z: 4, core: 2. Of those that a mesh axis runs over, the one named last changes fastest.
Arguments:
- byte_feats: bfloat16 [8, 2048, 768], P('wshard', 'ctx'), may hold values from -6 to 6
- lengths: int32 [8], P('wshard'), may hold values from 512 to 2048, as said below
- latent_array: bfloat16 [256, 1280], P('wshard'), may hold values from -6 to 6
- lat_gain: bfloat16 [1280], P('wshard'), may hold values from 0.5 to 1.5
- lat_bias: bfloat16 [1280], P('wshard'), may hold values from -4 to 4
- in_gain: bfloat16 [768], P('wshard'), may hold values from 0.5 to 1.5
- in_bias: bfloat16 [768], P('wshard'), may hold values from -4 to 4
- w_query: bfloat16 [1280, 256], P('wshard'), may hold values from -0.25 to 0.25
- w_key: bfloat16 [768, 256], P('wshard'), may hold values from -0.3125 to 0.3125
- w_value: bfloat16 [768, 1280], P('wshard'), may hold values from -0.21875 to 0.21875
- w_output: bfloat16 [1280, 1280], P('wshard'), may hold values from -2 to 2
- mlp_gain: bfloat16 [1280], P('wshard'), may hold values from 0.5 to 1.5
- mlp_bias: bfloat16 [1280], P('wshard'), may hold values from -4 to 4
- w_up: bfloat16 [1280, 1280], P('wshard'), may hold values from -0.15625 to 0.15625
- w_down: bfloat16 [1280, 1280], P('wshard'), may hold values from -0.15625 to 0.15625
- cotangent: bfloat16 [8, 256, 1280], P('wshard'), may hold values from -6 to 6
Outputs:
- latents_out: bfloat16 [8, 256, 1280], P('wshard')
- byte_grad: bfloat16 [8, 2048, 768], P('wshard', 'ctx')
- grad_latent: float32 [256, 1280], P('wshard')
- grad_lat_gain: float32 [1280], P('wshard')
- grad_lat_bias: float32 [1280], P('wshard')
- grad_in_gain: float32 [768], P('wshard')
- grad_in_bias: float32 [768], P('wshard')
- grad_query: float32 [1280, 256], P('wshard')
- grad_key: float32 [768, 256], P('wshard')
- grad_value: float32 [768, 1280], P('wshard')
- grad_output: float32 [1280, 1280], P('wshard')
- grad_mlp_gain: float32 [1280], P('wshard')
- grad_mlp_bias: float32 [1280], P('wshard')
- grad_up: float32 [1280, 1280], P('wshard')
- grad_down: float32 [1280, 1280], P('wshard')
Inputs may be any that keep to these rules, and one draw needn't show every extreme that they name: The first lengths[s] slots of sequence s hold bytes, the rest are padding; some sequence fills all 2048 slots.
All inputs are finite; a program needn't handle non-finite values.
Results may differ from a plain program's by a relative error of at most 0.019.
Values may be sent and summed in bfloat16 or wider, within the bound.
A program may use at most 256 MiB of HBM per device.

v0:
```python
import math
import jax
import jax.numpy as jnp
from jax import lax
from jax.sharding import PartitionSpec as P

H = 8


def layer_norm(values, gain, offset):
    center = jnp.mean(values, axis=-1, keepdims=True)
    centred = values - center
    variance = jnp.mean(centred * centred, axis=-1, keepdims=True)
    return centred * lax.rsqrt(variance + 1e-05) * gain + offset


def exact_gelu(values):
    return jax.nn.gelu(values, approximate=False)


def matmul(left, right):
    return jnp.dot(left, right, preferred_element_type=jnp.float32)


def combine(first, second):
    top_first, sum_first, num_first = first
    top_second, sum_second, num_second = second
    highest = jnp.maximum(top_first, top_second)
    weight_first = jnp.exp(top_first - highest)
    weight_second = jnp.exp(top_second - highest)
    return (
        highest,
        sum_first * weight_first + sum_second * weight_second,
        num_first * weight_first[..., None] + num_second * weight_second[..., None],
    )


def block_stats(queries, keys, values, start, length, score_scale):
    row_count = keys.shape[0]
    head_count = queries.shape[1]
    kheads = keys.reshape(row_count, head_count, -1)
    vheads = values.reshape(row_count, head_count, -1)
    scores = (
        jnp.einsum("lhd,khd->hlk", queries, kheads, preferred_element_type=jnp.float32)
        * score_scale
    )
    valid = start + lax.iota(jnp.int32, row_count) < length
    masked = jnp.where(valid, scores, -1e30)
    highest = jnp.max(masked, axis=-1)
    weights = jnp.where(valid, jnp.exp(masked - highest[..., None]), 0.0)
    numer = jnp.einsum(
        "hlk,khe->hle", weights.astype(jnp.bfloat16), vheads, preferred_element_type=jnp.float32
    )
    return (highest, jnp.sum(weights, axis=-1), numer)


def query_part(queries, grad_heads, log_total, delta, keys, values, start, length, score_scale):
    row_count = keys.shape[0]
    head_count = queries.shape[1]
    kheads = keys.reshape(row_count, head_count, -1)
    vheads = values.reshape(row_count, head_count, -1)
    scores = (
        jnp.einsum("lhd,khd->hlk", queries, kheads, preferred_element_type=jnp.float32)
        * score_scale
    )
    valid = start + lax.iota(jnp.int32, row_count) < length
    probs = jnp.where(valid, jnp.exp(scores - log_total[..., None]), 0.0)
    dprobs = jnp.einsum("lhe,khe->hlk", grad_heads, vheads, preferred_element_type=jnp.float32)
    dscores = (probs * (dprobs - delta[..., None])).astype(jnp.bfloat16)
    dquery = (
        jnp.einsum("hlk,khd->lhd", dscores, kheads, preferred_element_type=jnp.float32)
        * score_scale
    )
    return (dquery, dscores, probs)


def blocked(block_fn, carry, keys, values):
    row_count = keys.shape[0]
    block_size = math.gcd(row_count, 1024)
    block_count = row_count // block_size
    key_blocks = keys.reshape(block_count, block_size, keys.shape[1])
    value_blocks = values.reshape(block_count, block_size, values.shape[1])

    def scan_step(carried, block_item):
        key_block, value_block, offset = block_item
        return (block_fn(carried, key_block, value_block, offset * block_size), None)

    result, _ = lax.scan(
        scan_step, carry, (key_blocks, value_blocks, jnp.arange(block_count, dtype=jnp.int32))
    )
    return result


def shards(
    byte_feats,
    lengths,
    latent_array,
    lat_gain,
    lat_bias,
    in_gain,
    in_bias,
    w_query,
    w_key,
    w_value,
    w_output,
    mlp_gain,
    mlp_bias,
    w_up,
    w_down,
    cotangent,
):
    head_count = H
    micro_count = byte_feats.shape[0]
    slot_count = byte_feats.shape[1]
    key_start = lax.axis_index("ctx") * slot_count
    latent_outs = []
    byte_grads = []
    totals = None
    for micro_step in range(micro_count):
        gathered = (
            lax.all_gather(latent_array, "wshard", axis=0, tiled=True),
            lax.all_gather(lat_gain, "wshard", axis=0, tiled=True),
            lax.all_gather(lat_bias, "wshard", axis=0, tiled=True),
            lax.all_gather(in_gain, "wshard", axis=0, tiled=True),
            lax.all_gather(in_bias, "wshard", axis=0, tiled=True),
            lax.all_gather(w_query, "wshard", axis=0, tiled=True),
            lax.all_gather(w_key, "wshard", axis=0, tiled=True),
            lax.all_gather(w_value, "wshard", axis=0, tiled=True),
            lax.all_gather(w_output, "wshard", axis=0, tiled=True),
            lax.all_gather(mlp_gain, "wshard", axis=0, tiled=True),
            lax.all_gather(mlp_bias, "wshard", axis=0, tiled=True),
            lax.all_gather(w_up, "wshard", axis=0, tiled=True),
            lax.all_gather(w_down, "wshard", axis=0, tiled=True),
        )
        (
            latent,
            gain_lat,
            bias_lat,
            gain_in,
            bias_in,
            query_w,
            key_w,
            value_w,
            output_w,
            gain_mlp,
            bias_mlp,
            up_w,
            down_w,
        ) = gathered
        length = lengths[micro_step]
        features = byte_feats[micro_step].astype(jnp.float32)
        normed_in, in_back = jax.vjp(
            layer_norm, features, gain_in.astype(jnp.float32), bias_in.astype(jnp.float32)
        )
        input_low = normed_in.astype(jnp.bfloat16)
        keys = matmul(input_low, key_w).astype(jnp.bfloat16)
        values = matmul(input_low, value_w).astype(jnp.bfloat16)
        latent_full = latent.astype(jnp.float32)
        normed_lat, lat_back = jax.vjp(
            layer_norm, latent_full, gain_lat.astype(jnp.float32), bias_lat.astype(jnp.float32)
        )
        lat_low = normed_lat.astype(jnp.bfloat16)
        head_size = query_w.shape[1] // head_count
        score_scale = 1.0 / math.sqrt(head_size)
        queries = matmul(lat_low, query_w).astype(jnp.bfloat16).reshape(-1, head_count, head_size)
        lat_rows = queries.shape[0]
        value_head = values.shape[1] // head_count
        empty = (
            jnp.full((head_count, lat_rows), -1e30, jnp.float32),
            jnp.zeros((head_count, lat_rows), jnp.float32),
            jnp.zeros((head_count, lat_rows, value_head), jnp.float32),
        )

        def add_block(carried, key_block, value_block, block_start):
            return combine(
                carried,
                block_stats(queries, key_block, value_block, block_start, length, score_scale),
            )

        highest, total, numer = blocked(
            add_block,
            empty,
            lax.all_gather(keys, "ctx", axis=0, tiled=True),
            lax.all_gather(values, "ctx", axis=0, tiled=True),
        )
        attended = numer / total[..., None]
        log_total = highest + jnp.log(total)
        att_low = jnp.transpose(attended, (1, 0, 2)).reshape(lat_rows, -1).astype(jnp.bfloat16)
        hidden = latent_full + matmul(att_low, output_w)
        normed_mid, mid_back = jax.vjp(
            layer_norm, hidden, gain_mlp.astype(jnp.float32), bias_mlp.astype(jnp.float32)
        )
        mid_low = normed_mid.astype(jnp.bfloat16)
        upward = matmul(mid_low, up_w)
        activated, gelu_back = jax.vjp(exact_gelu, upward)
        act_low = activated.astype(jnp.bfloat16)
        result = hidden + matmul(act_low, down_w)
        latent_outs.append(result.astype(jnp.bfloat16))
        dout = cotangent[micro_step].astype(jnp.float32)
        dout_low = dout.astype(jnp.bfloat16)
        grad_down = matmul(act_low.T, dout_low)
        grad_act = matmul(dout_low, down_w.T)
        (grad_upward,) = gelu_back(grad_act)
        up_low = grad_upward.astype(jnp.bfloat16)
        grad_upw = matmul(mid_low.T, up_low)
        grad_mid = matmul(up_low, up_w.T)
        dhid_norm, grad_gmlp, grad_bmlp = mid_back(grad_mid)
        dhidden = dout + dhid_norm
        dhid_low = dhidden.astype(jnp.bfloat16)
        grad_outw = matmul(att_low.T, dhid_low)
        grad_att = matmul(dhid_low, output_w.T).astype(jnp.bfloat16)
        grad_heads = grad_att.reshape(lat_rows, head_count, value_head)
        delta = jnp.sum(
            jnp.transpose(grad_heads.astype(jnp.float32), (1, 0, 2)) * attended, axis=-1
        )
        dquery_local, dscores, probs = query_part(
            queries, grad_heads, log_total, delta, keys, values, key_start, length, score_scale
        )
        dkeys = (
            (
                jnp.einsum("hlk,lhd->khd", dscores, queries, preferred_element_type=jnp.float32)
                * score_scale
            )
            .astype(jnp.bfloat16)
            .reshape(slot_count, -1)
        )
        dvalues = (
            jnp.einsum(
                "hlk,lhe->khe",
                probs.astype(jnp.bfloat16),
                grad_heads,
                preferred_element_type=jnp.float32,
            )
            .astype(jnp.bfloat16)
            .reshape(slot_count, -1)
        )

        def fold_add_block(carried, key_block, value_block, block_start):
            return (
                carried
                + query_part(
                    queries,
                    grad_heads,
                    log_total,
                    delta,
                    key_block,
                    value_block,
                    block_start,
                    length,
                    score_scale,
                )[0]
            )

        dquery = blocked(
            fold_add_block,
            jnp.zeros((lat_rows, head_count, head_size), jnp.float32),
            lax.all_gather(keys, "ctx", axis=0, tiled=True),
            lax.all_gather(values, "ctx", axis=0, tiled=True),
        )
        dquery_low = dquery.reshape(lat_rows, -1).astype(jnp.bfloat16)
        grad_qw = matmul(lat_low.T, dquery_low)
        dnorm_lat = matmul(dquery_low, query_w.T)
        dlat_norm, grad_glat, grad_blat = lat_back(dnorm_lat)
        grad_lat = dhidden + dlat_norm
        grad_kw = matmul(input_low.T, dkeys)
        grad_vw = matmul(input_low.T, dvalues)
        dnorm_in = matmul(dkeys, key_w.T) + matmul(dvalues, value_w.T)
        dfeatures, grad_gin, grad_bin = in_back(dnorm_in)
        byte_grads.append(dfeatures.astype(jnp.bfloat16))
        step_grads = [
            grad_lat,
            grad_glat,
            grad_blat,
            grad_gin,
            grad_bin,
            grad_qw,
            grad_kw,
            grad_vw,
            grad_outw,
            grad_gmlp,
            grad_bmlp,
            grad_upw,
            grad_down,
        ]
        if totals is None:
            totals = step_grads
        else:
            totals = [older + newer for older, newer in zip(totals, step_grads)]
    shares = (
        lax.psum_scatter(
            totals[0].astype(jnp.bfloat16), "wshard", scatter_dimension=0, tiled=True
        ).astype(jnp.float32),
        lax.psum_scatter(
            totals[1].astype(jnp.bfloat16), "wshard", scatter_dimension=0, tiled=True
        ).astype(jnp.float32),
        lax.psum_scatter(
            totals[2].astype(jnp.bfloat16), "wshard", scatter_dimension=0, tiled=True
        ).astype(jnp.float32),
        lax.psum_scatter(
            totals[3].astype(jnp.bfloat16), "wshard", scatter_dimension=0, tiled=True
        ).astype(jnp.float32),
        lax.psum_scatter(
            totals[4].astype(jnp.bfloat16), "wshard", scatter_dimension=0, tiled=True
        ).astype(jnp.float32),
        lax.psum_scatter(
            totals[5].astype(jnp.bfloat16), "wshard", scatter_dimension=0, tiled=True
        ).astype(jnp.float32),
        lax.psum_scatter(
            totals[6].astype(jnp.bfloat16), "wshard", scatter_dimension=0, tiled=True
        ).astype(jnp.float32),
        lax.psum_scatter(
            totals[7].astype(jnp.bfloat16), "wshard", scatter_dimension=0, tiled=True
        ).astype(jnp.float32),
        lax.psum_scatter(
            totals[8].astype(jnp.bfloat16), "wshard", scatter_dimension=0, tiled=True
        ).astype(jnp.float32),
        lax.psum_scatter(
            totals[9].astype(jnp.bfloat16), "wshard", scatter_dimension=0, tiled=True
        ).astype(jnp.float32),
        lax.psum_scatter(
            totals[10].astype(jnp.bfloat16), "wshard", scatter_dimension=0, tiled=True
        ).astype(jnp.float32),
        lax.psum_scatter(
            totals[11].astype(jnp.bfloat16), "wshard", scatter_dimension=0, tiled=True
        ).astype(jnp.float32),
        lax.psum_scatter(
            totals[12].astype(jnp.bfloat16), "wshard", scatter_dimension=0, tiled=True
        ).astype(jnp.float32),
    )
    summed = (
        lax.psum(shares[3].astype(jnp.bfloat16), "ctx").astype(jnp.float32),
        lax.psum(shares[4].astype(jnp.bfloat16), "ctx").astype(jnp.float32),
        lax.psum(shares[6].astype(jnp.bfloat16), "ctx").astype(jnp.float32),
        lax.psum(shares[7].astype(jnp.bfloat16), "ctx").astype(jnp.float32),
    )
    return (
        jnp.stack(latent_outs),
        jnp.stack(byte_grads),
        shares[0],
        shares[1],
        shares[2],
        summed[0],
        summed[1],
        shares[5],
        summed[2],
        summed[3],
        shares[8],
        shares[9],
        shares[10],
        shares[11],
        shares[12],
    )


def solution(mesh):
    placed = (
        P("wshard", "ctx", None),
        P("wshard"),
        P("wshard", None),
        P("wshard"),
        P("wshard"),
        P("wshard"),
        P("wshard"),
        P("wshard", None),
        P("wshard", None),
        P("wshard", None),
        P("wshard", None),
        P("wshard"),
        P("wshard"),
        P("wshard", None),
        P("wshard", None),
        P("wshard", None, None),
    )
    return jax.shard_map(
        shards,
        mesh=mesh,
        in_specs=placed,
        out_specs=(
            P("wshard", None, None),
            P("wshard", "ctx", None),
            P("wshard", None),
            P("wshard"),
            P("wshard"),
            P("wshard"),
            P("wshard"),
            P("wshard", None),
            P("wshard", None),
            P("wshard", None),
            P("wshard", None),
            P("wshard"),
            P("wshard"),
            P("wshard", None),
            P("wshard", None),
        ),
        check_vma=False,
    )
```

profile of v0, /device:TPU:0, one launch (start us, length us, event | category | flops | bytes accessed | tf_op | source)
XLA Modules:
  0.0 846.3 jit_solution(12040518271220998177)
XLA Ops:
  15.8 21.7 %all-reduce.15 = (bf16[768]{0:T(1024)(128)(2,1)S(1)}, bf16[768]{0:T(1024)(128)(2,1)S(1)}, bf16[1280]{0:T(1024)(128)(2,1)S(1)}, bf16[1280]{0:T(1024)(128)(2,1)S(1...) all-reduce(bf16[768]{0:T(1024)(128)(2,1)S(1)} %dynamic-update-slice, ...), channel_id=1, replica_groups=mesh['ctx'=8,'wshard'=4] {'wshard'}, use_global_device_ids=true, to_apply=%add.1 | all-reduce | flops 6656 | bytes 26624
  38.8 17.7 %all_gather.71 = bf16[768,256]{1,0:T(8,128)(2,1)S(1)} all-gather(bf16[192,256]{1,0:T(8,128)(2,1)S(1)} %copy-done.57), channel_id=1, replica_groups=mesh['ctx'=8,'wshard'=4] {'wshard'}, dimensions={0}, use_global_device_ids=true | all-gather | bytes 491520 | tf_op jit(solution)/shard_map/all_gather | solution.py:127
  59.3 3.7 all-gather.11.cloned.1.call-done
  63.1 3.3 convolution_convert_fusion
  71.0 17.1 %all_gather.68 = bf16[256,1280]{1,0:T(8,128)(2,1)S(1)} all-gather(bf16[64,1280]{1,0:T(8,128)(2,1)S(1)} %copy-done.53), channel_id=1, replica_groups=mesh['ctx'=8,'wshard'=4] {'wshard'}, dimensions={0}, use_global_device_ids=true | all-gather | bytes 819200 | tf_op jit(solution)/shard_map/all_gather | solution.py:121
  88.6 15.9 %all_gather.75 = bf16[1280,256]{1,0:T(8,128)(2,1)S(1)} all-gather(bf16[320,256]{1,0:T(8,128)(2,1)S(1)} %copy-done.54), channel_id=1, replica_groups=mesh['ctx'=8,'wshard'=4] {'wshard'}, dimensions={0}, use_global_device_ids=true | all-gather | bytes 819200 | tf_op jit(solution)/shard_map/all_gather | solution.py:126
  108.4 5.1 all-gather.9.cloned.1.call-done
  119.2 37.8 %all-gather.23.cloned.1.call-done = bf16[2048,1280]{1,0:T(8,128)(2,1)} async-done(((bf16[256,1280]{1,0:T(8,128)(2,1)}), bf16[2048,1280]{1,0:T(8,128)(2,1)}) %all-gather.23.cloned.1.call-update) | async-done | bytes 5242896 | tf_op jit(solution)/shard_map/all_gather | solution.py:184
  157.0 8.1 copy.70
  165.1 35.3 %all-gather.13.cloned.1.call-done = bf16[2048,1280]{1,0:T(8,128)(2,1)} async-done(((bf16[256,1280]{1,0:T(8,128)(2,1)}), bf16[2048,1280]{1,0:T(8,128)(2,1)}) %all-gather.13.cloned.1.call-update) | async-done | bytes 5242896 | tf_op jit(solution)/shard_map/all_gather | solution.py:184
  200.4 8.0 copy.68
  208.4 25.4 %while.53 = (s32[]{:T(128)}, f32[8,256]{1,0:T(8,128)S(1)}, f32[8,256]{1,0:T(8,128)S(1)}, f32[8,256,160]{1,2,0:T(8,128)}, s32[2]{0:T(128)S(1)}, /*index=5*/s32[]{...) while((s32[]{:T(128)}, f32[8,256]{1,0:T(8,128)S(1)}, ...), condition=%wide.region_15.16_spmd.clone, body=%wide.region_12.15_spmd.clone.sunk | while | flops 833894400 | bytes 47960292 | solution.py:88
  210.3 2.2 constant_dynamic-slice_fusion.19
  212.5 2.3 bitcast_reduce_fusion.5
  214.9 2.6 fusion.322
  217.5 2.6 fusion.324
  225.1 2.3 bitcast_reduce_fusion.5
  227.5 2.6 fusion.322
  230.1 2.6 fusion.324
  234.8 25.6 %while.52 = (s32[]{:T(128)}, f32[8,256]{1,0:T(8,128)S(1)}, f32[8,256]{1,0:T(8,128)S(1)}, f32[8,256,160]{1,2,0:T(8,128)}, s32[2]{0:T(128)S(1)}, /*index=5*/s32[]{...) while((s32[]{:T(128)}, f32[8,256]{1,0:T(8,128)S(1)}, ...), condition=%wide.region_7.8_spmd.clone, body=%wide.region_4.7_spmd.clone.sunk | while | flops 833894400 | bytes 47960292 | solution.py:88
  238.8 2.3 bitcast_reduce_fusion.4
  241.1 2.6 fusion.315
  243.7 2.6 fusion.317
  251.5 2.3 bitcast_reduce_fusion.4
  253.8 2.6 fusion.315
  256.4 2.6 fusion.317
  260.4 2.3 fusion.149
  262.7 4.9 all-gather.15.cloned.1.call-done
  267.5 3.4 fusion.196
  275.5 58.0 %all-gather.17.cloned.1.call-done = bf16[1280,1280]{1,0:T(8,128)(2,1)} async-done(((bf16[320,1280]{1,0:T(8,128)(2,1)}), bf16[1280,1280]{1,0:T(8,128)(2,1)}) %all-gather.17.cloned.1.call-update) | async-done | bytes 3276816 | tf_op jit(solution)/shard_map/all_gather | solution.py:132
  333.4 7.7 multiply_convert_fusion.18
  341.2 5.4 multiply_convert_fusion.19
  346.6 52.8 %all-gather.19.cloned.1.call-done = bf16[1280,1280]{1,0:T(8,128)(2,1)} async-done(((bf16[320,1280]{1,0:T(8,128)(2,1)}), bf16[1280,1280]{1,0:T(8,128)(2,1)}) %all-gather.19.cloned.1.call-update) | async-done | bytes 3276816 | tf_op jit(solution)/shard_map/all_gather | solution.py:133
  399.3 4.2 add_convert_fusion.2
  427.6 34.5 %while.55 = (s32[]{:T(128)}, f32[256,8,32]{0,2,1:T(8,128)S(1)}, bf16[2,1024,256]{1,2,0:T(8,128)(2,1)}, s32[2]{0:T(128)S(1)}, s32[]{:T(128)}, /*index=5*/bf16[256...) while((s32[]{:T(128)}, f32[256,8,32]{0,2,1:T(8,128)S(1)}, ...), condition=%wide.region_33.34_spmd.clone, body=%wide.region_32.33_spmd.clone.sunk | while | flops 952305664 | bytes 27543732 | solution.py:88
  433.5 4.7 fusion.337
  438.3 6.7 fusion.338
  450.7 4.7 fusion.337
  455.5 6.7 fusion.338
  464.1 2.6 fusion.98
  466.8 2.3 fusion.174
  471.2 2.6 fusion.99
  473.9 2.5 fusion.95
  479.4 2.2 fusion.57
  482.6 30.5 %while.54 = (s32[]{:T(128)}, f32[256,8,32]{0,2,1:T(8,128)S(1)}, bf16[2,1024,256]{1,2,0:T(8,128)(2,1)S(1)}, s32[2]{0:T(128)S(1)}, s32[]{:T(128)}, /*index=5*/bf16...) while((s32[]{:T(128)}, f32[256,8,32]{0,2,1:T(8,128)S(1)}, ...), condition=%wide.region_29.30_spmd.clone, body=%wide.region_28.29_spmd.clone.sunk | while | flops 952305664 | bytes 27543732 | solution.py:88
  486.8 4.8 fusion.330
  491.6 6.4 fusion.331
  501.9 4.8 fusion.330
  506.7 6.4 fusion.331
  523.0 5.2 fusion.178
  528.2 9.5 %reduce-scatter.14.cloned.1.call-done = bf16[192,1280]{1,0:T(8,128)(2,1)} async-done(((bf16[768,1280]{1,0:T(8,128)(2,1)}), bf16[192,1280]{1,0:T(8,128)(2,1)}) %reduce-scatter.14.cloned.1.call-update) | async-done | bytes 491536 | tf_op jit(solution)/shard_map/reduce_scatter | solution.py:311
  537.9 5.7 fusion.55
  546.9 2.8 fusion.54
  550.8 2.3 fusion.143
  553.1 2.8 fusion.56
  562.5 17.7 %all-reduce.14 = (bf16[1280]{0:T(1024)(128)(2,1)S(1)}, bf16[1280]{0:T(1024)(128)(2,1)S(1)}, bf16[768]{0:T(1024)(128)(2,1)S(1)}, bf16[768]{0:T(1024)(128)(2,1)S(1...) all-reduce(bf16[1280]{0:T(1024)(128)(2,1)S(1)} %add_convert_fusion., ...), channel_id=3, replica_groups=mesh['ctx'=8,'wshard'=4] {'wshard'}, use_global_device_ids=true, to_apply=%region_39.40.clone | all-reduce | flops 6656 | bytes 26624
  580.4 12.0 %all-reduce.12 = (bf16[192]{0:T(256)(128)(2,1)S(1)}, bf16[192]{0:T(256)(128)(2,1)S(1)}) all-reduce(bf16[192]{0:T(256)(128)(2,1)S(1)} %dynamic-slice.11, bf16[192]{0:T(256)(128)(2,1)S(1)} %dynamic-slice.13), channel_id=1, replica_groups=mesh['ctx'=8,'wshard'=4] {'ctx'}, use_global_device_ids=true, to_apply=%region_46.47 | all-reduce | flops 384 | bytes 1536 | tf_op jit(solution)/shard_map/psum | solution.py:331
  607.2 36.8 %all-reduce.18.cloned.1.call-done = (bf16[192,256]{1,0:T(8,128)(2,1)}, bf16[192,1280]{1,0:T(8,128)(2,1)}) async-done(((bf16[192,256]{1,0:T(8,128)(2,1)}, bf16[192,1280]{1,0:T(8,128)(2,1)}), (bf16[192,256]{1,0:T(8,128)(2,1)}, bf16[192,1280]{1,0:T(8,128)(2,1)})) %all-reduce.18.cloned.1.call-update) | async-done | bytes 589840 | tf_op jit(solution)/shard_map/psum | solution.py:333
  647.6 60.1 %reduce-scatter.18.cloned.1.call-done = bf16[320,1280]{1,0:T(8,128)(2,1)} async-done(((bf16[1280,1280]{1,0:T(8,128)(2,1)}), bf16[320,1280]{1,0:T(8,128)(2,1)}) %reduce-scatter.18.cloned.1.call-update) | async-done | bytes 819216 | tf_op jit(solution)/shard_map/reduce_scatter | solution.py:323
  707.7 2.4 convert_element_type.382
  710.1 62.2 %reduce-scatter.16.cloned.1.call-done = bf16[320,1280]{1,0:T(8,128)(2,1)} async-done(((bf16[1280,1280]{1,0:T(8,128)(2,1)}), bf16[320,1280]{1,0:T(8,128)(2,1)}) %reduce-scatter.16.cloned.1.call-update) | async-done | bytes 819216 | tf_op jit(solution)/shard_map/reduce_scatter | solution.py:314
  772.3 2.4 convert_element_type.376
  774.8 62.2 %reduce-scatter.20.cloned.1.call-done = bf16[320,1280]{1,0:T(8,128)(2,1)} async-done(((bf16[1280,1280]{1,0:T(8,128)(2,1)}), bf16[320,1280]{1,0:T(8,128)(2,1)}) %reduce-scatter.20.cloned.1.call-update) | async-done | bytes 819216 | tf_op jit(solution)/shard_map/reduce_scatter | solution.py:326
  836.9 2.4 convert_element_type.384
  (455 shorter events, 132.5 us)
Async XLA Ops:
  7.2 49.4 %copy-start.3 = (bf16[2,256,768]{2,1,0:T(8,128)(2,1)S(1)}, bf16[2,256,768]{2,1,0:T(8,128)(2,1)}, u32[]{:S(2)}) copy-start(bf16[2,256,768]{2,1,0:T(8,128)(2,1)} %param.24) | copy-start | bytes 2359300
  7.2 31.6 %copy-start.57 = (bf16[192,256]{1,0:T(8,128)(2,1)S(1)}, bf16[192,256]{1,0:T(8,128)(2,1)}, u32[]{:S(2)}) copy-start(bf16[192,256]{1,0:T(8,128)(2,1)} %param.32) | copy-start | bytes 294916
  7.2 55.9 %all-gather.11.cloned.1.call-start = ((), (), s32[]{:S(2)}) async-start(), calls=%async_computation.8 | async-start | bytes 2457600 | tf_op jit(solution)/shard_map/all_gather | solution.py:128
  7.9 99.1 %all-gather.21.cloned.1.call-start = ((), (), s32[]{:S(2)}) async-start(), calls=%async_computation.13 | async-start | bytes 1179648 | tf_op jit(solution)/shard_map/all_gather | solution.py:183
  37.5 28.9 %copy-start.65 = (f32[768]{0:T(1024)}, f32[768]{0:T(1024)S(1)}, u32[]{:S(2)}) copy-start(f32[768]{0:T(1024)S(1)} %convert_element_type.302) | copy-start | bytes 9220
  37.5 28.9 %copy-start.60 = (f32[768]{0:T(1024)}, f32[768]{0:T(1024)S(1)}, u32[]{:S(2)}) copy-start(f32[768]{0:T(1024)S(1)} %convert_element_type.301) | copy-start | bytes 9220
  56.5 6.6 copy-start.78
  56.5 9.9 %copy-start.81 = (f32[256]{0:T(256)}, f32[256]{0:T(256)S(1)}, u32[]{:S(2)}) copy-start(f32[256]{0:T(256)S(1)} %get-tuple-element.636) | copy-start | bytes 3076
  56.9 6.1 copy-start.87
  58.1 55.4 %all-gather.9.cloned.1.call-start = ((), (), s32[]{:S(2)}) async-start(), calls=%async_computation.7 | async-start | bytes 1179648 | tf_op jit(solution)/shard_map/all_gather | solution.py:183
  58.1 8.3 copy-start.90
  59.3 97.7 %all-gather.23.cloned.1.call-start = ((), (), s32[]{:S(2)}) async-start(), calls=%async_computation.14 | async-start | bytes 5898240 | tf_op jit(solution)/shard_map/all_gather | solution.py:184
  63.1 3.4 copy-start.37
  66.4 134.0 %all-gather.13.cloned.1.call-start = ((), (), s32[]{:S(2)}) async-start(), calls=%async_computation.9 | async-start | bytes 5898240 | tf_op jit(solution)/shard_map/all_gather | solution.py:184
  68.1 2.9 copy-start.53
  68.1 199.4 %all-gather.15.cloned.1.call-start = ((), (), s32[]{:S(2)}) async-start(), calls=%async_computation.10 | async-start | bytes 4096000 | tf_op jit(solution)/shard_map/all_gather | solution.py:129
  68.7 264.7 %all-gather.17.cloned.1.call-start = ((), (), s32[]{:S(2)}) async-start(), calls=%async_computation.11 | async-start | bytes 4096000 | tf_op jit(solution)/shard_map/all_gather | solution.py:132
  69.5 329.9 %all-gather.19.cloned.1.call-start = ((), (), s32[]{:S(2)}) async-start(), calls=%async_computation.12 | async-start | bytes 4096000 | tf_op jit(solution)/shard_map/all_gather | solution.py:133
  70.2 18.4 %copy-start.54 = (bf16[320,256]{1,0:T(8,128)(2,1)S(1)}, bf16[320,256]{1,0:T(8,128)(2,1)}, u32[]{:S(2)}) copy-start(bf16[320,256]{1,0:T(8,128)(2,1)} %param.31) | copy-start | bytes 491524
  70.2 458.0 %reduce-scatter.12.cloned.1.call-start = ((), (), s32[]{:S(2)}) async-start(), calls=%async_computation.17 | async-start | bytes 491520 | tf_op jit(solution)/shard_map/reduce_scatter | solution.py:308
  71.0 35.5 %copy-start.48 = (f32[1280]{0:T(1024)}, f32[1280]{0:T(1024)S(1)}, u32[]{:S(2)}) copy-start(f32[1280]{0:T(1024)S(1)} %convert_element_type.305) | copy-start | bytes 15364
  71.0 35.5 %copy-start.58 = (f32[1280]{0:T(1024)}, f32[1280]{0:T(1024)S(1)}, u32[]{:S(2)}) copy-start(f32[1280]{0:T(1024)S(1)} %convert_element_type.306) | copy-start | bytes 15364
  88.3 18.8 %copy-start.63 = (f32[256]{0:T(256)}, f32[256]{0:T(256)S(1)}, u32[]{:S(2)}) copy-start(f32[256]{0:T(256)S(1)} %broadcast_multiply_fusion.2) | copy-start | bytes 3076
  88.6 18.4 %copy-start.97 = (f32[256]{0:T(256)}, f32[256]{0:T(256)S(1)}, u32[]{:S(2)}) copy-start(f32[256]{0:T(256)S(1)} %fusion.80) | copy-start | bytes 3076
  88.6 18.4 %copy-start.75 = (f32[256]{0:T(256)}, f32[256]{0:T(256)S(1)}, u32[]{:S(2)}) copy-start(f32[256]{0:T(256)S(1)} %fusion.162) | copy-start | bytes 3076
  104.6 3.8 copy-start.17
  214.9 2.6 copy-start.23
  267.5 5.3 copy-start.118
  270.9 138.7 %copy-start.1 = (f32[256,1280]{1,0:T(8,128)}, f32[256,1280]{1,0:T(8,128)S(1)}, u32[]{:S(2)}) copy-start(f32[256,1280]{1,0:T(8,128)S(1)} %get-tuple-element.630) | copy-start | bytes 3932164
  271.0 138.7 %copy-start.77 = (f32[256]{0:T(256)}, f32[256]{0:T(256)S(1)}, u32[]{:S(2)}) copy-start(f32[256]{0:T(256)S(1)} %broadcast_multiply_fusion.1) | copy-start | bytes 3076
  274.1 135.6 %copy-start.84 = (f32[256]{0:T(256)}, f32[256]{0:T(256)S(1)}, u32[]{:S(2)}) copy-start(f32[256]{0:T(256)S(1)} %broadcast_multiply_fusion) | copy-start | bytes 3076
  275.4 134.3 %copy-start.86 = (f32[256]{0:T(256)}, f32[256]{0:T(256)S(1)}, u32[]{:S(2)}) copy-start(f32[256]{0:T(256)S(1)} %fusion.163) | copy-start | bytes 3076
  275.4 134.3 %copy-start.99 = (f32[256]{0:T(256)}, f32[256]{0:T(256)S(1)}, u32[]{:S(2)}) copy-start(f32[256]{0:T(256)S(1)} %fusion.165) | copy-start | bytes 3076
  275.4 143.7 %copy-start.105 = (f32[8,256]{1,0:T(8,128)}, f32[8,256]{1,0:T(8,128)S(1)}, u32[]{:S(2)}) copy-start(f32[8,256]{1,0:T(8,128)S(1)} %log_add_fusion.1) | copy-start | bytes 24580
  333.4 7.7 copy-start.121
  399.3 4.2 copy-start.122
  399.3 5.3 copy-start.123
  399.3 5.3 copy-start.124
  403.6 2.6 copy-start.116
  410.5 3.3 copy-start.119
  411.9 9.4 %copy-start.32 = (bf16[256,1280]{1,0:T(8,128)(2,1)}, bf16[256,1280]{1,0:T(8,128)(2,1)S(1)}, u32[]{:S(2)}) copy-start(bf16[256,1280]{1,0:T(8,128)(2,1)S(1)} %get-tuple-element.611) | copy-start | bytes 1966084
  419.9 2.9 copy-start.120
  427.6 36.5 %copy-start.67 = (f32[8,256]{1,0:T(8,128)S(1)}, f32[8,256]{1,0:T(8,128)}, u32[]{:S(2)}) copy-start(f32[8,256]{1,0:T(8,128)} %fusion.84) | copy-start | bytes 24580
  464.1 2.7 copy-start.61
  464.1 2.7 copy-start.66
  464.1 2.7 copy-start.82
  464.1 2.7 copy-start.91
  471.2 2.6 copy-start.79
  471.2 2.7 copy-start.88
  473.8 4.7 copy-start.46
  476.4 61.4 %reduce-scatter.14.cloned.1.call-start = ((), (), s32[]{:S(2)}) async-start(), calls=%async_computation.18 | async-start | bytes 2457600 | tf_op jit(solution)/shard_map/reduce_scatter | solution.py:311
  481.7 122.2 %reduce-scatter.8.cloned.1.call-start = ((), (), s32[]{:S(2)}) async-start(), calls=%async_computation.15 | async-start | bytes 819200 | tf_op jit(solution)/shard_map/reduce_scatter | solution.py:290
  515.8 3.1 copy-start.15
  520.9 84.6 %reduce-scatter.10.cloned.1.call-start = ((), (), s32[]{:S(2)}) async-start(), calls=%async_computation.16 | async-start | bytes 819200 | tf_op jit(solution)/shard_map/reduce_scatter | solution.py:305
  522.9 14.9 %copy-start.42 = (bf16[256,1280]{1,0:T(8,128)(2,1)S(1)}, bf16[256,1280]{1,0:T(8,128)(2,1)}, u32[]{:S(2)}) copy-start(bf16[256,1280]{1,0:T(8,128)(2,1)} %copy-done.41) | copy-start | bytes 1966084
  522.9 14.9 %copy-start.85 = (f32[256]{0:T(256)S(1)}, f32[256]{0:T(256)}, u32[]{:S(2)}) copy-start(f32[256]{0:T(256)} %copy-done.84) | copy-start | bytes 3076
  522.9 14.9 %copy-start.100 = (f32[256]{0:T(256)S(1)}, f32[256]{0:T(256)}, u32[]{:S(2)}) copy-start(f32[256]{0:T(256)} %copy-done.99) | copy-start | bytes 3076
  522.9 121.0 %all-reduce.18.cloned.1.call-start = ((), (), s32[]{:S(2)}) async-start(), calls=%async_computation.22 | async-start | bytes 1179648 | tf_op jit(solution)/shard_map/psum | solution.py:333
  523.0 14.9 %copy-start.8 = (f32[256,1280]{1,0:T(8,128)S(1)}, f32[256,1280]{1,0:T(8,128)}, u32[]{:S(2)}) copy-start(f32[256,1280]{1,0:T(8,128)} %copy-done.6) | copy-start | bytes 3932164
  537.8 169.9 %reduce-scatter.18.cloned.1.call-start = ((), (), s32[]{:S(2)}) async-start(), calls=%async_computation.20 | async-start | bytes 4096000 | tf_op jit(solution)/shard_map/reduce_scatter | solution.py:323
  543.6 228.7 %reduce-scatter.16.cloned.1.call-start = ((), (), s32[]{:S(2)}) async-start(), calls=%async_computation.19 | async-start | bytes 4096000 | tf_op jit(solution)/shard_map/reduce_scatter | solution.py:314
  549.7 287.2 %reduce-scatter.20.cloned.1.call-start = ((), (), s32[]{:S(2)}) async-start(), calls=%async_computation.21 | async-start | bytes 4096000 | tf_op jit(solution)/shard_map/reduce_scatter | solution.py:326
  560.4 35.7 %copy-start.96 = (f32[256]{0:T(256)S(1)}, f32[256]{0:T(256)}, u32[]{:S(2)}) copy-start(f32[256]{0:T(256)} %copy-done.95) | copy-start | bytes 3076
  560.4 35.7 %copy-start.94 = (f32[256]{0:T(256)S(1)}, f32[256]{0:T(256)}, u32[]{:S(2)}) copy-start(f32[256]{0:T(256)} %copy-done.93) | copy-start | bytes 3076
  (81 other events, 132.1 us)
Sparse Core Ops, SparseCore 0:
  9.6 53.4 all-gather.10
  65.5 22.4 all-gather.20
  89.9 23.5 all-gather.8
  115.8 41.1 all-gather.22
  159.3 41.1 all-gather.12
  201.8 65.6 all-gather.14
  269.1 64.2 all-gather.16
  335.0 64.2 all-gather.18
  476.5 19.2 reduce-scatter.11
  498.0 39.6 reduce-scatter.13
  540.7 21.3 reduce-scatter.7
  565.0 21.3 reduce-scatter.9
  589.9 54.0 all-reduce.17
  646.1 61.5 reduce-scatter.17
  709.9 62.4 reduce-scatter.15
  774.5 62.3 reduce-scatter.19
where the time goes:
time: 854 us; the launch traced here: 846 us
  waiting for transfers between devices  431 us (50%)
  matrix products  153 us (18%)
  blocking collectives  102 us (12%)
  local copies, waits for them, and re-layouts  79.7 us (9%)
  other arithmetic  54.5 us (6%)
  between operations  18.7 us (2%)
    dot_general x35, matrix products, matmul(): return jnp.dot(left, right, preferred_element_type=jnp.float32)  76.7 us
    all_gather x2, waiting for transfers between devices, shards(): lax.all_gather(values, 'ctx', axis=0, tiled=True)  73.1 us
    reduce_scatter x1, waiting for transfers between devices, shards(): lax.psum_scatter(totals[8].astype(jnp.bfloat16), 'wshard', scatter_dimens...  62.2 us
    reduce_scatter x1, waiting for transfers between devices, shards(): lax.psum_scatter(totals[12].astype(jnp.bfloat16), 'wshard', scatter_dimen...  62.2 us
    reduce_scatter x1, waiting for transfers between devices, shards(): lax.psum_scatter(totals[11].astype(jnp.bfloat16), 'wshard', scatter_dimen...  60.1 us
    all_gather x1, waiting for transfers between devices, shards(): lax.all_gather(w_up, 'wshard', axis=0, tiled=True)  58 us
    all_gather x1, waiting for transfers between devices, shards(): lax.all_gather(w_down, 'wshard', axis=0, tiled=True)  52.8 us
    unnamed x259, local copies, waits for them, and re-layouts  40.3 us
  transfers between devices with their start and end apart: 16, of which 12 were waited for; matrix products, arithmetic and copies ran while one was open for 23% of the time, Pallas kernels for 0%

commit v1 on v0

--- a/solution.py
+++ b/solution.py
@@ -330,7 +330,7 @@
     summed = (
         lax.psum(shares[3].astype(jnp.bfloat16), "ctx").astype(jnp.float32),
         lax.psum(shares[4].astype(jnp.bfloat16), "ctx").astype(jnp.float32),
-        lax.psum(shares[6].astype(jnp.bfloat16), "ctx").astype(jnp.float32),
+        jnp.sum(lax.all_gather(shares[6].astype(jnp.bfloat16), "ctx"), axis=0).astype(jnp.float32),
         lax.psum(shares[7].astype(jnp.bfloat16), "ctx").astype(jnp.float32),
     )
     return (

time: 854 us -> 855 us (level)
  waiting for transfers between devices: 431 us -> 417 us
  blocking collectives: 102 us -> 112 us
    all_gather x0 -> x1, blocking collectives: none -> 10.6 us  [shards(): lax.all_gather(shares[6].astype(jnp.bfloat16), 'ctx')]
    reduce_scatter x1, waiting for transfers between devices: 9.55 us -> 0.01 us  [shards(): lax.psum_scatter(totals[7].astype(jnp.bfloat16), 'wshard', scatter_dimens...]
    unnamed x259 -> x263, local copies, waits for them, and re-layouts: 40.3 us -> 39.4 us
  transfers between devices with their start and end apart: 16 -> 16, of which waited for: 12 -> 11; matrix products, arithmetic and copies ran while one was open for 23% -> 24% of each run, Pallas kernels for 0% -> 0%
where the time goes in v1:
time: 855 us; the launch traced here: 847 us
  waiting for transfers between devices  417 us (49%)
  matrix products  155 us (18%)
  blocking collectives  112 us (13%)
  local copies, waits for them, and re-layouts  80.7 us (9%)
  other arithmetic  55.8 us (7%)
  between operations  19 us (2%)
    dot_general x35, matrix products, matmul(): return jnp.dot(left, right, preferred_element_type=jnp.float32)  79 us
    all_gather x2, waiting for transfers between devices, shards(): lax.all_gather(values, 'ctx', axis=0, tiled=True)  73.1 us
    reduce_scatter x1, waiting for transfers between devices, shards(): lax.psum_scatter(totals[11].astype(jnp.bfloat16), 'wshard', scatter_dimen...  62.5 us
    reduce_scatter x1, waiting for transfers between devices, shards(): lax.psum_scatter(totals[12].astype(jnp.bfloat16), 'wshard', scatter_dimen...  62.2 us
    reduce_scatter x1, waiting for transfers between devices, shards(): lax.psum_scatter(totals[8].astype(jnp.bfloat16), 'wshard', scatter_dimens...  62.2 us
    all_gather x1, waiting for transfers between devices, shards(): lax.all_gather(w_up, 'wshard', axis=0, tiled=True)  58 us
    all_gather x1, waiting for transfers between devices, shards(): lax.all_gather(w_down, 'wshard', axis=0, tiled=True)  52.7 us
    unnamed x263, local copies, waits for them, and re-layouts  39.4 us
  transfers between devices with their start and end apart: 16, of which 11 were waited for; matrix products, arithmetic and copies ran while one was open for 24% of the time, Pallas kernels for 0%

profile of v1, /device:TPU:0, one launch (start us, length us, event | category | flops | bytes accessed | tf_op | source)
XLA Modules:
  0.0 846.8 jit_solution(8827915949448471814)
XLA Ops:
  15.8 21.7 %all-reduce.14 = (bf16[768]{0:T(1024)(128)(2,1)S(1)}, bf16[768]{0:T(1024)(128)(2,1)S(1)}, bf16[1280]{0:T(1024)(128)(2,1)S(1)}, bf16[1280]{0:T(1024)(128)(2,1)S(1...) all-reduce(bf16[768]{0:T(1024)(128)(2,1)S(1)} %dynamic-update-slice, ...), channel_id=1, replica_groups=mesh['ctx'=8,'wshard'=4] {'wshard'}, use_global_device_ids=true, to_apply=%add.1 | all-reduce | flops 6656 | bytes 26624
  38.9 17.7 %all_gather.77 = bf16[768,256]{1,0:T(8,128)(2,1)S(1)} all-gather(bf16[192,256]{1,0:T(8,128)(2,1)S(1)} %copy-done.59), channel_id=1, replica_groups=mesh['ctx'=8,'wshard'=4] {'wshard'}, dimensions={0}, use_global_device_ids=true | all-gather | bytes 491520 | tf_op jit(solution)/shard_map/all_gather | solution.py:127
  59.4 3.7 all-gather.12.cloned.1.call-done
  63.1 3.3 convolution_convert_fusion
  71.1 17.1 %all_gather.74 = bf16[256,1280]{1,0:T(8,128)(2,1)S(1)} all-gather(bf16[64,1280]{1,0:T(8,128)(2,1)S(1)} %copy-done.55), channel_id=1, replica_groups=mesh['ctx'=8,'wshard'=4] {'wshard'}, dimensions={0}, use_global_device_ids=true | all-gather | bytes 819200 | tf_op jit(solution)/shard_map/all_gather | solution.py:121
  88.7 15.9 %all_gather.81 = bf16[1280,256]{1,0:T(8,128)(2,1)S(1)} all-gather(bf16[320,256]{1,0:T(8,128)(2,1)S(1)} %copy-done.56), channel_id=1, replica_groups=mesh['ctx'=8,'wshard'=4] {'wshard'}, dimensions={0}, use_global_device_ids=true | all-gather | bytes 819200 | tf_op jit(solution)/shard_map/all_gather | solution.py:126
  108.5 5.0 all-gather.10.cloned.1.call-done
  119.2 37.8 %all-gather.24.cloned.1.call-done = bf16[2048,1280]{1,0:T(8,128)(2,1)} async-done(((bf16[256,1280]{1,0:T(8,128)(2,1)}), bf16[2048,1280]{1,0:T(8,128)(2,1)}) %all-gather.24.cloned.1.call-update) | async-done | bytes 5242896 | tf_op jit(solution)/shard_map/all_gather | solution.py:184
  157.0 8.2 copy.70
  165.1 35.3 %all-gather.14.cloned.1.call-done = bf16[2048,1280]{1,0:T(8,128)(2,1)} async-done(((bf16[256,1280]{1,0:T(8,128)(2,1)}), bf16[2048,1280]{1,0:T(8,128)(2,1)}) %all-gather.14.cloned.1.call-update) | async-done | bytes 5242896 | tf_op jit(solution)/shard_map/all_gather | solution.py:184
  200.4 7.9 copy.68
  208.3 25.5 %while.53 = (s32[]{:T(128)}, f32[8,256]{1,0:T(8,128)S(1)}, f32[8,256]{1,0:T(8,128)S(1)}, f32[8,256,160]{1,2,0:T(8,128)}, s32[2]{0:T(128)S(1)}, /*index=5*/s32[]{...) while((s32[]{:T(128)}, f32[8,256]{1,0:T(8,128)S(1)}, ...), condition=%wide.region_15.16_spmd.clone, body=%wide.region_12.15_spmd.clone.sunk | while | flops 833894400 | bytes 47960292 | solution.py:88
  212.5 2.3 bitcast_reduce_fusion.5
  214.9 2.6 fusion.322
  217.5 2.6 fusion.324
  225.2 2.3 bitcast_reduce_fusion.5
  227.5 2.6 fusion.322
  230.1 2.6 fusion.324
  234.8 25.5 %while.52 = (s32[]{:T(128)}, f32[8,256]{1,0:T(8,128)S(1)}, f32[8,256]{1,0:T(8,128)S(1)}, f32[8,256,160]{1,2,0:T(8,128)}, s32[2]{0:T(128)S(1)}, /*index=5*/s32[]{...) while((s32[]{:T(128)}, f32[8,256]{1,0:T(8,128)S(1)}, ...), condition=%wide.region_7.8_spmd.clone, body=%wide.region_4.7_spmd.clone.sunk | while | flops 833894400 | bytes 47960292 | solution.py:88
  238.7 2.3 bitcast_reduce_fusion.4
  241.1 2.6 fusion.315
  243.7 2.6 fusion.317
  251.4 2.3 bitcast_reduce_fusion.4
  253.7 2.6 fusion.315
  256.3 2.6 fusion.317
  260.3 2.3 fusion.149
  262.6 5.0 all-gather.16.cloned.1.call-done
  267.5 3.4 fusion.196
  275.4 58.0 %all-gather.18.cloned.1.call-done = bf16[1280,1280]{1,0:T(8,128)(2,1)} async-done(((bf16[320,1280]{1,0:T(8,128)(2,1)}), bf16[1280,1280]{1,0:T(8,128)(2,1)}) %all-gather.18.cloned.1.call-update) | async-done | bytes 3276816 | tf_op jit(solution)/shard_map/all_gather | solution.py:132
  333.4 7.8 multiply_convert_fusion.18
  341.2 5.4 multiply_convert_fusion.19
  346.6 52.7 %all-gather.20.cloned.1.call-done = bf16[1280,1280]{1,0:T(8,128)(2,1)} async-done(((bf16[320,1280]{1,0:T(8,128)(2,1)}), bf16[1280,1280]{1,0:T(8,128)(2,1)}) %all-gather.20.cloned.1.call-update) | async-done | bytes 3276816 | tf_op jit(solution)/shard_map/all_gather | solution.py:133
  399.3 4.2 add_convert_fusion.2
  429.3 34.8 %while.55 = (s32[]{:T(128)}, f32[256,8,32]{0,2,1:T(8,128)S(1)}, bf16[2,1024,256]{1,2,0:T(8,128)(2,1)}, s32[2]{0:T(128)S(1)}, s32[]{:T(128)}, /*index=5*/bf16[256...) while((s32[]{:T(128)}, f32[256,8,32]{0,2,1:T(8,128)S(1)}, ...), condition=%wide.region_33.34_spmd.clone, body=%wide.region_32.33_spmd.clone.sunk | while | flops 952305664 | bytes 27543732 | solution.py:88
  435.2 4.8 fusion.337
  440.0 6.7 fusion.338
  452.6 4.8 fusion.337
  457.4 6.7 fusion.338
  469.6 33.1 %while.54 = (s32[]{:T(128)}, f32[256,8,32]{0,2,1:T(8,128)S(1)}, bf16[2,1024,256]{1,2,0:T(8,128)(2,1)S(1)}, s32[2]{0:T(128)S(1)}, s32[]{:T(128)}, /*index=5*/bf16...) while((s32[]{:T(128)}, f32[256,8,32]{0,2,1:T(8,128)S(1)}, ...), condition=%wide.region_29.30_spmd.clone, body=%wide.region_28.29_spmd.clone.sunk | while | flops 952305664 | bytes 27543732 | solution.py:88
  472.5 2.3 constant_dynamic-slice_fusion.21
  474.8 4.8 fusion.330
  479.6 6.8 fusion.331
  491.1 4.8 fusion.330
  495.9 6.7 fusion.331
  510.1 3.2 fusion.98
  513.3 2.5 fusion.174
  515.8 3.0 fusion.99
  518.8 2.7 fusion.95
  521.6 3.5 add_convert_fusion
  528.3 5.1 fusion.178
  533.5 5.9 fusion.55
  542.7 2.7 fusion.54
  546.5 2.3 fusion.143
  548.8 2.8 fusion.56
  558.3 16.1 %all-reduce.13 = (bf16[1280]{0:T(1024)(128)(2,1)S(1)}, bf16[1280]{0:T(1024)(128)(2,1)S(1)}, bf16[768]{0:T(1024)(128)(2,1)S(1)}, bf16[768]{0:T(1024)(128)(2,1)S(1...) all-reduce(bf16[1280]{0:T(1024)(128)(2,1)S(1)} %add_convert_fusion., ...), channel_id=4, replica_groups=mesh['ctx'=8,'wshard'=4] {'wshard'}, use_global_device_ids=true, to_apply=%region_39.40.clone | all-reduce | flops 6656 | bytes 26624
  574.6 12.6 %all-reduce.12 = (bf16[192]{0:T(256)(128)(2,1)S(1)}, bf16[192]{0:T(256)(128)(2,1)S(1)}) all-reduce(bf16[192]{0:T(256)(128)(2,1)S(1)} %dynamic-slice.11, bf16[192]{0:T(256)(128)(2,1)S(1)} %dynamic-slice.13), channel_id=1, replica_groups=mesh['ctx'=8,'wshard'=4] {'ctx'}, use_global_device_ids=true, to_apply=%region_46.47 | all-reduce | flops 384 | bytes 1536 | tf_op jit(solution)/shard_map/psum | solution.py:331
  598.7 10.6 %all-gather = bf16[1536,256]{1,0:T(8,128)(2,1)S(1)} all-gather(bf16[192,256]{1,0:T(8,128)(2,1)} %reduce-scatter.12.cloned.1.call-done), channel_id=2, replica_groups=mesh['ctx'=8,'wshard'=4] {'ctx'}, dimensions={0}, use_global_device_ids=true | all-gather | bytes 884736 | tf_op jit(solution)/shard_map/all_gather | solution.py:333
  613.4 30.1 %all-reduce.17.cloned.1.call-done = bf16[192,1280]{1,0:T(8,128)(2,1)} async-done(((bf16[192,1280]{1,0:T(8,128)(2,1)}), bf16[192,1280]{1,0:T(8,128)(2,1)}) %all-reduce.17.cloned.1.call-update) | async-done | bytes 491536 | tf_op jit(solution)/shard_map/psum | solution.py:334
  645.6 62.5 %reduce-scatter.18.cloned.1.call-done = bf16[320,1280]{1,0:T(8,128)(2,1)} async-done(((bf16[1280,1280]{1,0:T(8,128)(2,1)}), bf16[320,1280]{1,0:T(8,128)(2,1)}) %reduce-scatter.18.cloned.1.call-update) | async-done | bytes 819216 | tf_op jit(solution)/shard_map/reduce_scatter | solution.py:323
  708.1 2.4 convert_element_type.384
  710.5 62.2 %reduce-scatter.16.cloned.1.call-done = bf16[320,1280]{1,0:T(8,128)(2,1)} async-done(((bf16[1280,1280]{1,0:T(8,128)(2,1)}), bf16[320,1280]{1,0:T(8,128)(2,1)}) %reduce-scatter.16.cloned.1.call-update) | async-done | bytes 819216 | tf_op jit(solution)/shard_map/reduce_scatter | solution.py:314
  772.7 2.4 convert_element_type.378
  775.1 62.2 %reduce-scatter.20.cloned.1.call-done = bf16[320,1280]{1,0:T(8,128)(2,1)} async-done(((bf16[1280,1280]{1,0:T(8,128)(2,1)}), bf16[320,1280]{1,0:T(8,128)(2,1)}) %reduce-scatter.20.cloned.1.call-update) | async-done | bytes 819216 | tf_op jit(solution)/shard_map/reduce_scatter | solution.py:326
  837.3 2.4 convert_element_type.386
  (461 shorter events, 133.5 us)
Async XLA Ops:
  7.2 49.4 %copy-start.3 = (bf16[2,256,768]{2,1,0:T(8,128)(2,1)S(1)}, bf16[2,256,768]{2,1,0:T(8,128)(2,1)}, u32[]{:S(2)}) copy-start(bf16[2,256,768]{2,1,0:T(8,128)(2,1)} %param.24) | copy-start | bytes 2359300
  7.2 31.7 %copy-start.59 = (bf16[192,256]{1,0:T(8,128)(2,1)S(1)}, bf16[192,256]{1,0:T(8,128)(2,1)}, u32[]{:S(2)}) copy-start(bf16[192,256]{1,0:T(8,128)(2,1)} %param.32) | copy-start | bytes 294916
  7.2 55.9 %all-gather.12.cloned.1.call-start = ((), (), s32[]{:S(2)}) async-start(), calls=%async_computation.8 | async-start | bytes 2457600 | tf_op jit(solution)/shard_map/all_gather | solution.py:128
  7.9 99.2 %all-gather.22.cloned.1.call-start = ((), (), s32[]{:S(2)}) async-start(), calls=%async_computation.13 | async-start | bytes 1179648 | tf_op jit(solution)/shard_map/all_gather | solution.py:183
  37.6 28.8 %copy-start.70 = (f32[768]{0:T(1024)}, f32[768]{0:T(1024)S(1)}, u32[]{:S(2)}) copy-start(f32[768]{0:T(1024)S(1)} %convert_element_type.304) | copy-start | bytes 9220
  37.6 28.8 %copy-start.64 = (f32[768]{0:T(1024)}, f32[768]{0:T(1024)S(1)}, u32[]{:S(2)}) copy-start(f32[768]{0:T(1024)S(1)} %convert_element_type.303) | copy-start | bytes 9220
  56.6 6.5 copy-start.83
  56.6 9.8 %copy-start.86 = (f32[256]{0:T(256)}, f32[256]{0:T(256)S(1)}, u32[]{:S(2)}) copy-start(f32[256]{0:T(256)S(1)} %get-tuple-element.634) | copy-start | bytes 3076
  57.0 6.0 copy-start.93
  58.1 55.4 %all-gather.10.cloned.1.call-start = ((), (), s32[]{:S(2)}) async-start(), calls=%async_computation.7 | async-start | bytes 1179648 | tf_op jit(solution)/shard_map/all_gather | solution.py:183
  58.2 8.2 copy-start.96
  59.4 97.6 %all-gather.24.cloned.1.call-start = ((), (), s32[]{:S(2)}) async-start(), calls=%async_computation.14 | async-start | bytes 5898240 | tf_op jit(solution)/shard_map/all_gather | solution.py:184
  63.1 3.4 copy-start.37
  66.4 134.0 %all-gather.14.cloned.1.call-start = ((), (), s32[]{:S(2)}) async-start(), calls=%async_computation.9 | async-start | bytes 5898240 | tf_op jit(solution)/shard_map/all_gather | solution.py:184
  68.1 2.9 copy-start.55
  68.1 199.4 %all-gather.16.cloned.1.call-start = ((), (), s32[]{:S(2)}) async-start(), calls=%async_computation.10 | async-start | bytes 4096000 | tf_op jit(solution)/shard_map/all_gather | solution.py:129
  68.7 264.7 %all-gather.18.cloned.1.call-start = ((), (), s32[]{:S(2)}) async-start(), calls=%async_computation.11 | async-start | bytes 4096000 | tf_op jit(solution)/shard_map/all_gather | solution.py:132
  69.5 329.9 %all-gather.20.cloned.1.call-start = ((), (), s32[]{:S(2)}) async-start(), calls=%async_computation.12 | async-start | bytes 4096000 | tf_op jit(solution)/shard_map/all_gather | solution.py:133
  70.2 18.5 %copy-start.56 = (bf16[320,256]{1,0:T(8,128)(2,1)S(1)}, bf16[320,256]{1,0:T(8,128)(2,1)}, u32[]{:S(2)}) copy-start(bf16[320,256]{1,0:T(8,128)(2,1)} %param.31) | copy-start | bytes 491524
  70.2 463.2 %reduce-scatter.14.cloned.1.call-start = ((), (), s32[]{:S(2)}) async-start(), calls=%async_computation.18 | async-start | bytes 2457600 | tf_op jit(solution)/shard_map/reduce_scatter | solution.py:311
  71.0 35.5 %copy-start.50 = (f32[1280]{0:T(1024)}, f32[1280]{0:T(1024)S(1)}, u32[]{:S(2)}) copy-start(f32[1280]{0:T(1024)S(1)} %convert_element_type.307) | copy-start | bytes 15364
  71.0 270.2 %copy-start.60 = (f32[1280]{0:T(1024)}, f32[1280]{0:T(1024)S(1)}, u32[]{:S(2)}) copy-start(f32[1280]{0:T(1024)S(1)} %convert_element_type.316) | copy-start | bytes 15364
  71.1 35.5 %copy-start.62 = (f32[1280]{0:T(1024)}, f32[1280]{0:T(1024)S(1)}, u32[]{:S(2)}) copy-start(f32[1280]{0:T(1024)S(1)} %convert_element_type.308) | copy-start | bytes 15364
  88.3 18.8 %copy-start.67 = (f32[256]{0:T(256)}, f32[256]{0:T(256)S(1)}, u32[]{:S(2)}) copy-start(f32[256]{0:T(256)S(1)} %broadcast_multiply_fusion.2) | copy-start | bytes 3076
  88.6 18.5 %copy-start.103 = (f32[256]{0:T(256)}, f32[256]{0:T(256)S(1)}, u32[]{:S(2)}) copy-start(f32[256]{0:T(256)S(1)} %fusion.80) | copy-start | bytes 3076
  88.7 18.4 %copy-start.78 = (f32[256]{0:T(256)}, f32[256]{0:T(256)S(1)}, u32[]{:S(2)}) copy-start(f32[256]{0:T(256)S(1)} %fusion.162) | copy-start | bytes 3076
  104.6 2.5 copy-start.17
  214.8 2.6 copy-start.23
  227.5 2.6 copy-start.23
  241.1 2.6 copy-start.21
  253.7 2.6 copy-start.21
  267.5 5.3 copy-start.120
  270.9 138.7 %copy-start.1 = (f32[256,1280]{1,0:T(8,128)}, f32[256,1280]{1,0:T(8,128)S(1)}, u32[]{:S(2)}) copy-start(f32[256,1280]{1,0:T(8,128)S(1)} %get-tuple-element.628) | copy-start | bytes 3932164
  271.0 138.7 %copy-start.81 = (f32[256]{0:T(256)}, f32[256]{0:T(256)S(1)}, u32[]{:S(2)}) copy-start(f32[256]{0:T(256)S(1)} %broadcast_multiply_fusion.1) | copy-start | bytes 3076
  274.1 135.6 %copy-start.89 = (f32[256]{0:T(256)}, f32[256]{0:T(256)S(1)}, u32[]{:S(2)}) copy-start(f32[256]{0:T(256)S(1)} %broadcast_multiply_fusion) | copy-start | bytes 3076
  275.4 134.3 %copy-start.91 = (f32[256]{0:T(256)}, f32[256]{0:T(256)S(1)}, u32[]{:S(2)}) copy-start(f32[256]{0:T(256)S(1)} %fusion.163) | copy-start | bytes 3076
  275.4 134.3 %copy-start.106 = (f32[256]{0:T(256)}, f32[256]{0:T(256)S(1)}, u32[]{:S(2)}) copy-start(f32[256]{0:T(256)S(1)} %fusion.165) | copy-start | bytes 3076
  333.4 7.8 copy-start.123
  399.3 4.2 copy-start.124
  399.3 5.3 copy-start.125
  399.3 5.3 copy-start.126
  403.6 2.6 copy-start.118
  410.5 3.3 copy-start.121
  412.0 8.9 %copy-start.32 = (bf16[256,1280]{1,0:T(8,128)(2,1)}, bf16[256,1280]{1,0:T(8,128)(2,1)S(1)}, u32[]{:S(2)}) copy-start(bf16[256,1280]{1,0:T(8,128)(2,1)S(1)} %get-tuple-element.609) | copy-start | bytes 1966084
  419.3 2.9 copy-start.122
  429.2 34.9 %copy-start.65 = (f32[768]{0:T(1024)S(1)}, f32[768]{0:T(1024)}, u32[]{:S(2)}) copy-start(f32[768]{0:T(1024)} %copy-done.64) | copy-start | bytes 9220
  429.2 34.9 %copy-start.71 = (f32[768]{0:T(1024)S(1)}, f32[768]{0:T(1024)}, u32[]{:S(2)}) copy-start(f32[768]{0:T(1024)} %copy-done.70) | copy-start | bytes 9220
  429.2 34.9 %copy-start.87 = (f32[256]{0:T(256)S(1)}, f32[256]{0:T(256)}, u32[]{:S(2)}) copy-start(f32[256]{0:T(256)} %copy-done.86) | copy-start | bytes 3076
  429.2 34.9 %copy-start.97 = (f32[256]{0:T(256)S(1)}, f32[256]{0:T(256)}, u32[]{:S(2)}) copy-start(f32[256]{0:T(256)} %copy-done.96) | copy-start | bytes 3076
  468.7 130.0 %reduce-scatter.12.cloned.1.call-start = ((), (), s32[]{:S(2)}) async-start(), calls=%async_computation.17 | async-start | bytes 491520 | tf_op jit(solution)/shard_map/reduce_scatter | solution.py:308
  518.8 2.8 copy-start.10
  521.5 3.7 copy-start.42
  521.5 88.6 %reduce-scatter.8.cloned.1.call-start = ((), (), s32[]{:S(2)}) async-start(), calls=%async_computation.15 | async-start | bytes 819200 | tf_op jit(solution)/shard_map/reduce_scatter | solution.py:290
  525.1 86.6 %reduce-scatter.10.cloned.1.call-start = ((), (), s32[]{:S(2)}) async-start(), calls=%async_computation.16 | async-start | bytes 819200 | tf_op jit(solution)/shard_map/reduce_scatter | solution.py:305
  527.9 5.6 copy-start.44
  527.9 5.6 copy-start.90
  527.9 5.6 copy-start.107
  527.9 115.6 %all-reduce.17.cloned.1.call-start = ((), (), s32[]{:S(2)}) async-start(), calls=%async_computation.19 | async-start | bytes 983040 | tf_op jit(solution)/shard_map/psum | solution.py:334
  528.3 5.2 copy-start.8
  533.4 174.7 %reduce-scatter.18.cloned.1.call-start = ((), (), s32[]{:S(2)}) async-start(), calls=%async_computation.21 | async-start | bytes 4096000 | tf_op jit(solution)/shard_map/reduce_scatter | solution.py:323
  539.4 233.3 %reduce-scatter.16.cloned.1.call-start = ((), (), s32[]{:S(2)}) async-start(), calls=%async_computation.20 | async-start | bytes 4096000 | tf_op jit(solution)/shard_map/reduce_scatter | solution.py:314
  545.4 291.9 %reduce-scatter.20.cloned.1.call-start = ((), (), s32[]{:S(2)}) async-start(), calls=%async_computation.22 | async-start | bytes 4096000 | tf_op jit(solution)/shard_map/reduce_scatter | solution.py:326
  556.3 34.6 %copy-start.102 = (f32[256]{0:T(256)S(1)}, f32[256]{0:T(256)}, u32[]{:S(2)}) copy-start(f32[256]{0:T(256)} %copy-done.101) | copy-start | bytes 3076
  556.3 34.6 %copy-start.100 = (f32[256]{0:T(256)S(1)}, f32[256]{0:T(256)}, u32[]{:S(2)}) copy-start(f32[256]{0:T(256)} %copy-done.99) | copy-start | bytes 3076
  (83 other events, 136.0 us)
Sparse Core Ops, SparseCore 0:
  9.6 53.4 all-gather.11
  65.5 22.4 all-gather.21
  89.9 23.5 all-gather.9
  115.8 41.1 all-gather.23
  159.3 41.1 all-gather.13
  201.8 65.6 all-gather.15
  269.1 64.2 all-gather.17
  335.0 64.2 all-gather.19
  468.8 40.0 reduce-scatter.13
  521.6 18.9 reduce-scatter.11
  543.0 20.3 reduce-scatter.7
  566.2 21.0 reduce-scatter.9
  590.8 52.7 all-reduce.16
  645.7 62.3 reduce-scatter.17
  710.3 62.3 reduce-scatter.15
  774.9 62.3 reduce-scatter.19
